TPU v7x, 256 devices: a whole 4x4x8 slice. The times are simulated.
256 devices in a mesh: grid: 64 (over z, y, core), lev: 4 (over x).
Axes of the slice: x: 4, y: 4, z: 8, core: 2. Of those that a mesh axis runs over, the one named last changes fastest.
Arguments:
- prior_fields: float32 [128, 8, 32768], P('grid', 'lev'), may hold values from -6 to 6
- channel_weights: float32 [8, 4], P('lev'), may hold values from 0.1 to 1
- obs_owner: int32 [4], replicated, may hold values from 0 to 63
- obs_offset: int32 [4, 4, 64], replicated, may hold values from 0 to 511
- obs_value: float32 [4, 4, 64], P(None, 'lev'), may hold values from -30 to 30
- obs_error: float32 [4, 4, 64], P(None, 'lev'), may hold values from 0.5 to 2
- ancestors: int32 [4, 4, 64, 128], P(None, 'lev', 'grid'), may hold values from 0 to 127
Outputs:
- posterior_fields: float32 [128, 8, 32768], P('grid', 'lev')
All inputs are finite; a program needn't handle non-finite values.
Results may differ from a plain program's by a relative error of at most 0.0003.
Values sent between devices are 32-bit elements; how exact they have to be, the bound alone decides.
A program may use at most 128 MiB of HBM per device.

v0:
```python
import jax
import jax.numpy as jnp
from jax import lax
from jax.sharding import PartitionSpec as P

NB = 4
HIGH = lax.Precision.HIGHEST


def spread(value, axis, source):
    kept = jnp.where(lax.axis_index(axis) == source, value, 0).astype(value.dtype)
    return lax.psum(kept, axis)


def blend_matrices(prior_obs, observed, obs_dev, centres, positions, scale, parents):
    count = observed.shape[0]
    members = prior_obs.shape[1]
    innovation = ((observed[:, None] - prior_obs) / obs_dev[:, None]) ** 2
    distance = (centres[:, None] - positions[None, :]) / scale
    taper = jnp.exp(-0.5 * distance * distance)
    log_weight = -0.5 / count * jnp.dot(taper, innovation, precision=HIGH)
    top_value = jnp.max(log_weight, axis=1, keepdims=True)
    expo_weight = jnp.exp(log_weight - top_value)
    weight = expo_weight / jnp.sum(expo_weight, axis=1, keepdims=True)
    alpha = 0.8 * (1.0 - jnp.exp(-jnp.sum(taper, axis=1) / count))
    onehot = (parents[:, :, None] == jnp.arange(members, dtype=jnp.int32)[None, None, :]).astype(
        jnp.float32
    )
    identity = jnp.eye(members, dtype=jnp.float32)
    remain = 1.0 - alpha
    return (
        alpha[:, None, None] * onehot
        + remain[:, None, None] * identity[None]
        + (weight - 1.0 / members)[:, None, :]
    )


def body(prior_fields, channel_weights, obs_owner, obs_offset, obs_value, obs_error, ancestors):
    grid_count = lax.axis_size("grid")
    member_slab, group_depth, cells = prior_fields.shape
    members = member_slab * grid_count
    block_cells = cells // grid_count
    local_regions = ancestors.shape[2]
    region_cells = block_cells // local_regions
    scale = local_regions * grid_count / 2.0
    groups = channel_weights.shape[1]
    count = obs_offset.shape[2]
    group = lax.axis_index("lev")
    block = lax.axis_index("grid")
    region_list = jnp.arange(local_regions, dtype=jnp.int32)
    centres = (block * local_regions + region_list).astype(jnp.float32) + 0.5
    first_cells = obs_offset[0].reshape(-1)
    fields = lax.all_to_all(prior_fields, "grid", split_axis=2, concat_axis=0, tiled=True)
    picked = fields[:, :, first_cells]
    for batch in range(NB):
        owner = obs_owner[batch]
        if batch > 0:
            picked = fields[:, :, obs_offset[batch].reshape(-1)]
        partial_value = jnp.einsum(
            "mlgk,lg->gkm",
            picked.reshape(members, group_depth, groups, count),
            channel_weights,
            precision=HIGH,
        )
        shared = spread(partial_value, "grid", owner)
        priors = lax.psum(shared, "lev")
        own_priors = lax.dynamic_index_in_dim(priors, group, 0, keepdims=False)
        own_offsets = lax.dynamic_index_in_dim(obs_offset[batch], group, 0, keepdims=False)
        positions = (owner * block_cells + own_offsets).astype(jnp.float32) / region_cells
        blend = blend_matrices(
            own_priors,
            obs_value[batch, 0],
            obs_error[batch, 0],
            centres,
            positions,
            scale,
            ancestors[batch, 0],
        )
        slab = fields.reshape(members, group_depth, local_regions, region_cells)
        mixed = jnp.einsum("rjm,mlrc->jlrc", blend, slab, precision=HIGH)
        fields = mixed.reshape(members, group_depth, block_cells)
    return lax.all_to_all(fields, "grid", split_axis=0, concat_axis=2, tiled=True)


def solution(mesh):
    in_specs = (
        P("grid", "lev", None),
        P("lev", None),
        P(),
        P(),
        P(None, "lev", None),
        P(None, "lev", None),
        P(None, "lev", "grid", None),
    )
    out_specs = P("grid", "lev", None)
    return jax.shard_map(body, mesh=mesh, in_specs=in_specs, out_specs=out_specs, check_vma=False)
```

profile of v0, /device:TPU:1, one launch (start us, length us, event | category | flops | bytes accessed | tf_op | source)
XLA Modules:
  0.0 1151.4 jit_solution(4428390036950253252)
XLA Ops:
  6.5 32.4 %copy.30 = f32[2,2,32768]{1,0,2:T(2,128)} copy(f32[2,2,32768]{2,1,0:T(2,128)} %param.7) | data formatting | bytes 1048576 | tf_op args[0]
  39.0 49.5 %reshape.797 = f32[64,1,2048]{2,1,0:T(1,128)} reshape(f32[32768,2,2]{2,1,0:T(2,128)} %bitcast.174) | data formatting | bytes 1048576
  88.5 13.2 %all-to-all-start = ((f32[64,1,2048]{2,1,0:T(1,128)}), f32[64,1,2048]{2,1,0:T(1,128)S(1)}, u32[]{:S(2)}, u32[]{:S(2)}) async-start(f32[64,1,2048]{2,1,0:T(1,128)} %reshape.797), calls=%async_computation | async-start | bytes 1048576 | tf_op jit(solution)/shard_map/all_to_all | solution.py:53
  101.8 0.1 reshape_squeeze.13
  101.9 0.1 reshape_squeeze.12
  101.9 0.7 fusion.106
  103.3 16.1 %all-to-all-done = f32[64,1,2048]{2,1,0:T(1,128)S(1)} async-done(((f32[64,1,2048]{2,1,0:T(1,128)}), f32[64,1,2048]{2,1,0:T(1,128)S(1)}, u32[]{:S(2)}, u32[]{:S(2)}) %all-to-all-start) | async-done | bytes 524320 | tf_op jit(solution)/shard_map/all_to_all | solution.py:53
  119.4 0.5 broadcast.610
  119.9 1.9 reduce.32
  121.8 53.4 %reshape.798 = f32[32768,2,2]{2,1,0:T(2,128)} reshape(f32[64,2048]{1,0:T(8,128)S(1)} %reduce.32) | data formatting | bytes 1048576
  175.2 35.6 %copy.31 = f32[2,2,64,512]{3,0,2,1:T(2,128)S(1)} copy(f32[2,2,64,512]{1,0,3,2:T(2,128)} %bitcast.173) | data formatting | bytes 1048576 | tf_op jit(solution)/shard_map/all_to_all | solution.py:53
  210.9 0.4 all_to_all.29
  211.2 0.2 copy.32
  211.5 1.0 gather_fusion
  212.5 0.1 multiply_reduce_fusion.3
  212.6 0.7 select_bitcast_fusion.3
  213.3 0.0 all-reduce.11.cloned.1.call-start
  214.0 169.1 %all-reduce.9.cloned.1.call-done = f32[4,64,128]{2,1,0:T(8,128)} async-done(((f32[4,64,128]{2,1,0:T(8,128)}), f32[4,64,128]{2,1,0:T(8,128)}) %all-reduce.9.cloned.1.call-update) | async-done | bytes 131088 | tf_op jit(solution)/shard_map/psum | solution.py:12
  383.2 0.6 fusion.104
  385.2 0.1 reshape_squeeze.15
  385.3 0.1 reshape_squeeze.14
  385.4 41.5 %all-reduce.11.cloned.1.call-done = f32[4,64,128]{2,1,0:T(8,128)} async-done(((f32[4,64,128]{2,1,0:T(8,128)}), f32[4,64,128]{2,1,0:T(8,128)}) %all-reduce.11.cloned.1.call-update) | async-done | bytes 131088 | tf_op jit(solution)/shard_map/psum | solution.py:66
  426.9 1.6 fusion.107
  428.4 1.3 fusion.97
  429.8 1.3 divide_add_fusion.3
  431.1 0.6 fusion.7
  431.8 0.2 copy.34
  432.0 1.0 gather_fusion.1
  433.0 0.1 multiply_reduce_fusion.2
  433.1 0.7 select_bitcast_fusion.2
  434.5 175.3 %all-reduce.13.cloned.1.call-done = f32[4,64,128]{2,1,0:T(8,128)} async-done(((f32[4,64,128]{2,1,0:T(8,128)}), f32[4,64,128]{2,1,0:T(8,128)}) %all-reduce.13.cloned.1.call-update) | async-done | bytes 131088 | tf_op jit(solution)/shard_map/psum | solution.py:12
  609.8 0.2 all-reduce.17.cloned.1.call-start
  610.1 0.6 fusion.103
  610.7 0.1 copy.66
  612.1 41.4 %all-reduce.15.cloned.1.call-done = f32[4,64,128]{2,1,0:T(8,128)} async-done(((f32[4,64,128]{2,1,0:T(8,128)}), f32[4,64,128]{2,1,0:T(8,128)}) %all-reduce.15.cloned.1.call-update) | async-done | bytes 131088 | tf_op jit(solution)/shard_map/psum | solution.py:66
  653.5 1.6 fusion.108
  655.1 1.3 fusion.98
  656.4 1.3 divide_add_fusion.2
  657.8 1.0 convolution_bitcast_fusion.2
  658.8 0.4 copy.37
  659.2 1.0 gather_fusion.2
  660.2 0.4 multiply_reduce_fusion.1
  660.6 0.7 select_bitcast_fusion.1
  662.0 175.4 %all-reduce.17.cloned.1.call-done = f32[4,64,128]{2,1,0:T(8,128)} async-done(((f32[4,64,128]{2,1,0:T(8,128)}), f32[4,64,128]{2,1,0:T(8,128)}) %all-reduce.17.cloned.1.call-update) | async-done | bytes 131088 | tf_op jit(solution)/shard_map/psum | solution.py:12
  837.4 0.6 fusion.102
  839.4 41.5 %all-reduce.19.cloned.1.call-done = f32[4,64,128]{2,1,0:T(8,128)} async-done(((f32[4,64,128]{2,1,0:T(8,128)}), f32[4,64,128]{2,1,0:T(8,128)}) %all-reduce.19.cloned.1.call-update) | async-done | bytes 131088 | tf_op jit(solution)/shard_map/psum | solution.py:66
  880.9 1.6 fusion.109
  882.5 1.3 fusion.99
  883.9 1.3 divide_add_fusion.1
  885.2 0.7 convolution_bitcast_fusion.1
  885.9 0.4 copy.38
  886.3 1.0 gather_fusion.3
  887.3 0.4 multiply_reduce_fusion
  887.7 0.7 select_bitcast_fusion
  888.4 176.1 %all-reduce.21.cloned.1.call-done = f32[4,64,128]{2,1,0:T(8,128)} async-done(((f32[4,64,128]{2,1,0:T(8,128)}), f32[4,64,128]{2,1,0:T(8,128)}) %all-reduce.21.cloned.1.call-update) | async-done | bytes 131088 | tf_op jit(solution)/shard_map/psum | solution.py:12
  1065.2 0.6 fusion.101
  1066.5 41.8 %all-reduce.23.cloned.1.call-done = f32[4,64,128]{2,1,0:T(8,128)} async-done(((f32[4,64,128]{2,1,0:T(8,128)}), f32[4,64,128]{2,1,0:T(8,128)}) %all-reduce.23.cloned.1.call-update) | async-done | bytes 131088 | tf_op jit(solution)/shard_map/psum | solution.py:66
  1108.3 1.6 fusion.110
  1109.9 1.3 fusion.100
  1111.2 1.3 divide_add_fusion
  1112.6 0.7 convolution_bitcast_fusion
  1113.2 0.2 copy.39
  1113.5 30.3 %all_to_all.36 = f32[128,2,512]{2,1,0:T(2,128)S(1)} all-to-all(f32[128,2,512]{2,1,0:T(2,128)S(1)} %copy.39), channel_id=1, replica_groups=mesh['grid'=64,'lev'=4] {'grid'}, dimensions={0} | all-to-all | bytes 1048576 | tf_op jit(solution)/shard_map/all_to_all | solution.py:82
  1143.7 0.8 copy.67
  (37 shorter events, 0.5 us)
Async XLA Ops:
  39.0 62.8 %copy-start.1 = (s32[4,4,64]{2,1,0:T(4,128)S(1)}, s32[4,4,64]{2,1,0:T(4,128)}, u32[]{:S(2)}) copy-start(s32[4,4,64]{2,1,0:T(4,128)} %param.10) | copy-start | bytes 12292
  39.0 63.0 %copy-start.2 = (s32[4]{0:T(128)S(1)}, s32[4]{0:T(128)}, u32[]{:S(2)}) copy-start(s32[4]{0:T(128)} %param.9) | copy-start | bytes 52
  39.0 64.3 %copy-start.4 = (f32[4,1,64]{2,1,0:T(1,128)S(1)}, f32[4,1,64]{2,1,0:T(1,128)}, u32[]{:S(2)}) copy-start(f32[4,1,64]{2,1,0:T(1,128)} %param.12) | copy-start | bytes 3076
  39.0 64.3 %copy-start.5 = (f32[4,1,64]{2,1,0:T(1,128)S(1)}, f32[4,1,64]{2,1,0:T(1,128)}, u32[]{:S(2)}) copy-start(f32[4,1,64]{2,1,0:T(1,128)} %param.11) | copy-start | bytes 3076
  88.5 30.9 %all-to-all-start = ((f32[64,1,2048]{2,1,0:T(1,128)}), f32[64,1,2048]{2,1,0:T(1,128)S(1)}, u32[]{:S(2)}, u32[]{:S(2)}) async-start(f32[64,1,2048]{2,1,0:T(1,128)} %reshape.797), calls=%async_computation | async-start | bytes 1048576 | tf_op jit(solution)/shard_map/all_to_all | solution.py:53
  101.7 281.4 %all-reduce.9.cloned.1.call-start = ((), (), s32[]{:S(2)}) async-start(), calls=%async_computation.2 | async-start | bytes 262144 | tf_op jit(solution)/shard_map/psum | solution.py:12
  175.2 37.3 %copy-start = (f32[2,4]{1,0:T(2,128)S(1)}, f32[2,4]{1,0:T(2,128)}, u32[]{:S(2)}) copy-start(f32[2,4]{1,0:T(2,128)} %param.8) | copy-start | bytes 100
  175.2 38.1 %copy-start.3 = (s32[4,1,1,128]{3,2,1,0:T(1,128)S(1)}, s32[4,1,1,128]{3,2,1,0:T(1,128)}, u32[]{:S(2)}) copy-start(s32[4,1,1,128]{3,2,1,0:T(1,128)} %param.13) | copy-start | bytes 6148
  213.3 213.6 %all-reduce.11.cloned.1.call-start = ((), (), s32[]{:S(2)}) async-start(), calls=%async_computation.3 | async-start | bytes 262144 | tf_op jit(solution)/shard_map/psum | solution.py:66
  383.1 226.7 %all-reduce.13.cloned.1.call-start = ((), (), s32[]{:S(2)}) async-start(), calls=%async_computation.4 | async-start | bytes 262144 | tf_op jit(solution)/shard_map/psum | solution.py:12
  433.8 219.7 %all-reduce.15.cloned.1.call-start = ((), (), s32[]{:S(2)}) async-start(), calls=%async_computation.5 | async-start | bytes 262144 | tf_op jit(solution)/shard_map/psum | solution.py:66
  609.8 227.5 %all-reduce.17.cloned.1.call-start = ((), (), s32[]{:S(2)}) async-start(), calls=%async_computation.6 | async-start | bytes 262144 | tf_op jit(solution)/shard_map/psum | solution.py:12
  661.3 219.6 %all-reduce.19.cloned.1.call-start = ((), (), s32[]{:S(2)}) async-start(), calls=%async_computation.7 | async-start | bytes 262144 | tf_op jit(solution)/shard_map/psum | solution.py:66
  837.4 227.1 %all-reduce.21.cloned.1.call-start = ((), (), s32[]{:S(2)}) async-start(), calls=%async_computation.8 | async-start | bytes 262144 | tf_op jit(solution)/shard_map/psum | solution.py:12
  888.3 220.0 %all-reduce.23.cloned.1.call-start = ((), (), s32[]{:S(2)}) async-start(), calls=%async_computation.9 | async-start | bytes 262144 | tf_op jit(solution)/shard_map/psum | solution.py:66
Sparse Core Ops, SparseCore 0:
  213.4 169.6 all-reduce.8
  385.4 41.3 all-reduce.10
  433.9 175.8 all-reduce.12
  612.1 41.3 all-reduce.14
  661.4 175.8 all-reduce.16
  839.5 41.3 all-reduce.18
  888.5 175.9 all-reduce.20
  1066.9 41.3 all-reduce.22
where the time goes:
time: 1160 us; the launch traced here: 1150 us
  waiting for transfers between devices  878 us (76%)
  local copies, waits for them, and re-layouts  179 us (15%)
  blocking collectives  30.3 us (3%)
  between operations  21.8 us (2%)
  other arithmetic  18.7 us (2%)
  starting transfers between devices  13.7 us (1%)
    psum x4, waiting for transfers between devices, spread(): return lax.psum(kept, axis)  696 us
    psum x4, waiting for transfers between devices, body(): priors = lax.psum(shared, 'lev')  166 us
    unnamed x18, local copies, waits for them, and re-layouts  136 us
    all_to_all x4, local copies, waits for them, and re-layouts, body(): lax.all_to_all(prior_fields, 'grid', split_axis=2, concat_axis=0, tiled=T...  36.7 us
    all_to_all x1, blocking collectives, body(): lax.all_to_all(fields, 'grid', split_axis=0, concat_axis=2, tiled=True)  30.3 us
  transfers between devices with their start and end apart: 9, of which 9 were waited for; matrix products, arithmetic and copies ran while one was open for 0% of the time, Pallas kernels for 0%

commit v1 on v0

--- a/solution.py
+++ b/solution.py
@@ -9,7 +9,7 @@
 
 def spread(value, axis, source):
     kept = jnp.where(lax.axis_index(axis) == source, value, 0).astype(value.dtype)
-    return lax.psum(kept, axis)
+    return jnp.sum(lax.all_gather(kept, axis), axis=0)
 
 
 def blend_matrices(prior_obs, observed, obs_dev, centres, positions, scale, parents):

time: 1160 us -> 804 us (0.69)
  waiting for transfers between devices: 878 us -> 509 us
  other arithmetic: 18.7 us -> 36.8 us
    psum x4 -> x0, waiting for transfers between devices: 696 us -> none  [spread(): return lax.psum(kept, axis)]
    all_gather x0 -> x4, waiting for transfers between devices: none -> 336 us  [spread(): return jnp.sum(lax.all_gather(kept, axis), axis=0)]
    reduce_sum x0 -> x4, other arithmetic: none -> 18.1 us  [spread(): return jnp.sum(lax.all_gather(kept, axis), axis=0)]
where the time goes in v1:
time: 804 us; the launch traced here: 800 us
  waiting for transfers between devices  509 us (63%)
  local copies, waits for them, and re-layouts  179 us (22%)
  other arithmetic  36.8 us (5%)
  blocking collectives  30.3 us (4%)
  between operations  21.4 us (3%)
  starting transfers between devices  13.7 us (2%)
  matrix products  9.31 us (1%)
    all_gather x4, waiting for transfers between devices, spread(): return jnp.sum(lax.all_gather(kept, axis), axis=0)  336 us
    psum x4, waiting for transfers between devices, body(): priors = lax.psum(shared, 'lev')  157 us
    unnamed x18, local copies, waits for them, and re-layouts  136 us
    all_to_all x4, local copies, waits for them, and re-layouts, body(): lax.all_to_all(prior_fields, 'grid', split_axis=2, concat_axis=0, tiled=T...  36.8 us
    all_to_all x1, blocking collectives, body(): lax.all_to_all(fields, 'grid', split_axis=0, concat_axis=2, tiled=True)  30.3 us
    reduce_sum x4, other arithmetic, spread(): return jnp.sum(lax.all_gather(kept, axis), axis=0)  18.1 us
    all_to_all x1, waiting for transfers between devices, body(): lax.all_to_all(prior_fields, 'grid', split_axis=2, concat_axis=0, tiled=T...  16.2 us
  transfers between devices with their start and end apart: 9, of which 9 were waited for; matrix products, arithmetic and copies ran while one was open for 0% of the time, Pallas kernels for 0%

profile of v1, /device:TPU:1, one launch (start us, length us, event | category | flops | bytes accessed | tf_op | source)
XLA Modules:
  0.0 800.0 jit_solution(13077704125849972402)
XLA Ops:
  6.5 32.4 %copy.30 = f32[2,2,32768]{1,0,2:T(2,128)} copy(f32[2,2,32768]{2,1,0:T(2,128)} %param.7) | data formatting | bytes 1048576 | tf_op args[0]
  39.0 49.5 %reshape.801 = f32[64,1,2048]{2,1,0:T(1,128)} reshape(f32[32768,2,2]{2,1,0:T(2,128)} %bitcast.178) | data formatting | bytes 1048576
  88.5 13.2 %all-to-all-start = ((f32[64,1,2048]{2,1,0:T(1,128)}), f32[64,1,2048]{2,1,0:T(1,128)S(1)}, u32[]{:S(2)}, u32[]{:S(2)}) async-start(f32[64,1,2048]{2,1,0:T(1,128)} %reshape.801), calls=%async_computation | async-start | bytes 1048576 | tf_op jit(solution)/shard_map/all_to_all | solution.py:53
  101.7 0.1 reshape_squeeze.13
  101.9 0.7 fusion.106
  103.2 16.2 %all-to-all-done = f32[64,1,2048]{2,1,0:T(1,128)S(1)} async-done(((f32[64,1,2048]{2,1,0:T(1,128)}), f32[64,1,2048]{2,1,0:T(1,128)S(1)}, u32[]{:S(2)}, u32[]{:S(2)}) %all-to-all-start) | async-done | bytes 524320 | tf_op jit(solution)/shard_map/all_to_all | solution.py:53
  119.4 0.5 broadcast.610
  119.9 1.9 reduce.32
  121.8 53.4 %reshape.802 = f32[32768,2,2]{2,1,0:T(2,128)} reshape(f32[64,2048]{1,0:T(8,128)S(1)} %reduce.32) | data formatting | bytes 1048576
  175.2 35.7 %copy.31 = f32[2,2,64,512]{3,0,2,1:T(2,128)S(1)} copy(f32[2,2,64,512]{1,0,3,2:T(2,128)} %bitcast.177) | data formatting | bytes 1048576 | tf_op jit(solution)/shard_map/all_to_all | solution.py:53
  210.9 0.4 all_to_all.29
  211.2 0.2 copy.32
  211.5 1.0 gather_fusion
  212.5 0.1 multiply_reduce_fusion.3
  212.6 0.7 select_bitcast_fusion.3
  214.0 79.3 %all-gather.9.cloned.1.call-done = f32[256,64,128]{2,1,0:T(8,128)} async-done(((f32[4,64,128]{2,1,0:T(8,128)}), f32[256,64,128]{2,1,0:T(8,128)}) %all-gather.9.cloned.1.call-update) | async-done | bytes 8388624 | tf_op jit(solution)/shard_map/all_gather | solution.py:12
  293.3 4.5 reduce_sum.109
  297.8 0.6 fusion.104
  299.8 39.2 %all-reduce.5.cloned.1.call-done = f32[4,64,128]{2,1,0:T(8,128)} async-done(((f32[4,64,128]{2,1,0:T(8,128)}), f32[4,64,128]{2,1,0:T(8,128)}) %all-reduce.5.cloned.1.call-update) | async-done | bytes 131088 | tf_op jit(solution)/shard_map/psum | solution.py:66
  339.0 1.6 fusion.107
  340.6 1.3 fusion.97
  341.9 1.3 divide_add_fusion.3
  343.3 0.6 fusion.7
  343.9 0.2 copy.34
  344.2 1.0 gather_fusion.1
  345.2 0.1 multiply_reduce_fusion.2
  345.3 0.7 select_bitcast_fusion.2
  345.9 0.2 all-reduce.7.cloned.1.call-start
  347.0 85.1 %all-gather.11.cloned.1.call-done = f32[256,64,128]{2,1,0:T(8,128)} async-done(((f32[4,64,128]{2,1,0:T(8,128)}), f32[256,64,128]{2,1,0:T(8,128)}) %all-gather.11.cloned.1.call-update) | async-done | bytes 8388624 | tf_op jit(solution)/shard_map/all_gather | solution.py:12
  432.1 4.5 reduce_sum.112
  436.7 0.6 fusion.103
  437.3 0.1 copy.66
  438.6 39.2 %all-reduce.7.cloned.1.call-done = f32[4,64,128]{2,1,0:T(8,128)} async-done(((f32[4,64,128]{2,1,0:T(8,128)}), f32[4,64,128]{2,1,0:T(8,128)}) %all-reduce.7.cloned.1.call-update) | async-done | bytes 131088 | tf_op jit(solution)/shard_map/psum | solution.py:66
  477.9 1.6 fusion.108
  479.4 1.3 fusion.98
  480.8 1.3 divide_add_fusion.2
  482.1 1.0 convolution_bitcast_fusion.2
  483.2 0.4 copy.37
  483.6 1.0 gather_fusion.2
  484.6 0.4 multiply_reduce_fusion.1
  485.0 0.7 select_bitcast_fusion.1
  486.3 85.5 %all-gather.13.cloned.1.call-done = f32[256,64,128]{2,1,0:T(8,128)} async-done(((f32[4,64,128]{2,1,0:T(8,128)}), f32[256,64,128]{2,1,0:T(8,128)}) %all-gather.13.cloned.1.call-update) | async-done | bytes 8388624 | tf_op jit(solution)/shard_map/all_gather | solution.py:12
  571.8 4.5 reduce_sum.115
  576.4 0.6 fusion.102
  578.3 39.2 %all-reduce.9.cloned.1.call-done = f32[4,64,128]{2,1,0:T(8,128)} async-done(((f32[4,64,128]{2,1,0:T(8,128)}), f32[4,64,128]{2,1,0:T(8,128)}) %all-reduce.9.cloned.1.call-update) | async-done | bytes 131088 | tf_op jit(solution)/shard_map/psum | solution.py:66
  617.6 1.6 fusion.109
  619.1 1.3 fusion.99
  620.5 1.3 divide_add_fusion.1
  621.8 0.7 convolution_bitcast_fusion.1
  622.5 0.4 copy.38
  622.9 1.0 gather_fusion.3
  623.9 0.4 multiply_reduce_fusion
  624.3 0.7 select_bitcast_fusion
  625.0 86.1 %all-gather.15.cloned.1.call-done = f32[256,64,128]{2,1,0:T(8,128)} async-done(((f32[4,64,128]{2,1,0:T(8,128)}), f32[256,64,128]{2,1,0:T(8,128)}) %all-gather.15.cloned.1.call-update) | async-done | bytes 8388624 | tf_op jit(solution)/shard_map/all_gather | solution.py:12
  711.1 4.5 reduce_sum.118
  716.3 0.6 fusion.101
  717.6 39.3 %all-reduce.11.cloned.1.call-done = f32[4,64,128]{2,1,0:T(8,128)} async-done(((f32[4,64,128]{2,1,0:T(8,128)}), f32[4,64,128]{2,1,0:T(8,128)}) %all-reduce.11.cloned.1.call-update) | async-done | bytes 131088 | tf_op jit(solution)/shard_map/psum | solution.py:66
  756.9 1.6 fusion.110
  758.5 1.3 fusion.100
  759.8 1.3 divide_add_fusion
  761.2 0.7 convolution_bitcast_fusion
  761.8 0.2 copy.39
  762.0 30.3 %all_to_all.36 = f32[128,2,512]{2,1,0:T(2,128)S(1)} all-to-all(f32[128,2,512]{2,1,0:T(2,128)S(1)} %copy.39), channel_id=1, replica_groups=mesh['grid'=64,'lev'=4] {'grid'}, dimensions={0} | all-to-all | bytes 1048576 | tf_op jit(solution)/shard_map/all_to_all | solution.py:82
  792.3 0.8 copy.67
  (41 shorter events, 0.8 us)
Async XLA Ops:
  39.0 62.7 %copy-start.1 = (s32[4,4,64]{2,1,0:T(4,128)S(1)}, s32[4,4,64]{2,1,0:T(4,128)}, u32[]{:S(2)}) copy-start(s32[4,4,64]{2,1,0:T(4,128)} %param.10) | copy-start | bytes 12292
  39.0 62.9 %copy-start.2 = (s32[4]{0:T(128)S(1)}, s32[4]{0:T(128)}, u32[]{:S(2)}) copy-start(s32[4]{0:T(128)} %param.9) | copy-start | bytes 52
  88.5 30.9 %all-to-all-start = ((f32[64,1,2048]{2,1,0:T(1,128)}), f32[64,1,2048]{2,1,0:T(1,128)S(1)}, u32[]{:S(2)}, u32[]{:S(2)}) async-start(f32[64,1,2048]{2,1,0:T(1,128)} %reshape.801), calls=%async_computation | async-start | bytes 1048576 | tf_op jit(solution)/shard_map/all_to_all | solution.py:53
  101.7 191.6 %all-gather.9.cloned.1.call-start = ((), (), s32[]{:S(2)}) async-start(), calls=%async_computation.6 | async-start | bytes 8519680 | tf_op jit(solution)/shard_map/all_gather | solution.py:12
  175.2 37.3 %copy-start = (f32[2,4]{1,0:T(2,128)S(1)}, f32[2,4]{1,0:T(2,128)}, u32[]{:S(2)}) copy-start(f32[2,4]{1,0:T(2,128)} %param.8) | copy-start | bytes 100
  175.2 38.8 %copy-start.3 = (s32[4,1,1,128]{3,2,1,0:T(1,128)S(1)}, s32[4,1,1,128]{3,2,1,0:T(1,128)}, u32[]{:S(2)}) copy-start(s32[4,1,1,128]{3,2,1,0:T(1,128)} %param.13) | copy-start | bytes 6148
  175.2 38.8 %copy-start.4 = (f32[4,1,64]{2,1,0:T(1,128)S(1)}, f32[4,1,64]{2,1,0:T(1,128)}, u32[]{:S(2)}) copy-start(f32[4,1,64]{2,1,0:T(1,128)} %param.12) | copy-start | bytes 3076
  175.2 38.8 %copy-start.5 = (f32[4,1,64]{2,1,0:T(1,128)S(1)}, f32[4,1,64]{2,1,0:T(1,128)}, u32[]{:S(2)}) copy-start(f32[4,1,64]{2,1,0:T(1,128)} %param.11) | copy-start | bytes 3076
  213.3 125.7 %all-reduce.5.cloned.1.call-start = ((), (), s32[]{:S(2)}) async-start(), calls=%async_computation.2 | async-start | bytes 262144 | tf_op jit(solution)/shard_map/psum | solution.py:66
  297.8 134.3 %all-gather.11.cloned.1.call-start = ((), (), s32[]{:S(2)}) async-start(), calls=%async_computation.7 | async-start | bytes 8519680 | tf_op jit(solution)/shard_map/all_gather | solution.py:12
  345.9 131.9 %all-reduce.7.cloned.1.call-start = ((), (), s32[]{:S(2)}) async-start(), calls=%async_computation.3 | async-start | bytes 262144 | tf_op jit(solution)/shard_map/psum | solution.py:66
  436.6 135.2 %all-gather.13.cloned.1.call-start = ((), (), s32[]{:S(2)}) async-start(), calls=%async_computation.8 | async-start | bytes 8519680 | tf_op jit(solution)/shard_map/all_gather | solution.py:12
  485.6 131.9 %all-reduce.9.cloned.1.call-start = ((), (), s32[]{:S(2)}) async-start(), calls=%async_computation.4 | async-start | bytes 262144 | tf_op jit(solution)/shard_map/psum | solution.py:66
  576.4 134.8 %all-gather.15.cloned.1.call-start = ((), (), s32[]{:S(2)}) async-start(), calls=%async_computation.9 | async-start | bytes 8519680 | tf_op jit(solution)/shard_map/all_gather | solution.py:12
  625.0 131.9 %all-reduce.11.cloned.1.call-start = ((), (), s32[]{:S(2)}) async-start(), calls=%async_computation.5 | async-start | bytes 262144 | tf_op jit(solution)/shard_map/psum | solution.py:66
Sparse Core Ops, SparseCore 0:
  213.4 79.8 all-gather.8
  297.9 41.0 all-reduce.4
  346.1 85.9 all-gather.10
  436.8 41.0 all-reduce.6
  485.8 85.9 all-gather.12
  576.5 41.0 all-reduce.8
  625.1 85.9 all-gather.14
  715.8 41.0 all-reduce.10
